TPU v7x, 32 devices: a whole 2x2x4 slice. The times are simulated.
32 devices in a mesh: group: 2 (over x), shard: 16 (over z, y, core).
Axes of the slice: x: 2, y: 2, z: 4, core: 2. Of those that a mesh axis runs over, the one named last changes fastest.
Arguments:
- offer_attribute_matrix: bfloat16 [128, 128, 1024], P(('group', 'shard')), may hold values from -6 to 6
- kept_offers: int32 [128, 32], P(('group', 'shard')), may hold values from 0 to 127, as said below
- expert_target: int32 [128, 6], P(('group', 'shard')), may hold values from 0 to 15, all different within a row; in each aligned block of 4 rows (0 to 3, 4 to 7, ...) at most 3 rows name the same one
- sequence_extent: int32 [128], P(('group', 'shard')), may hold values from 1 to 128
- behaviour_sequence: bfloat16 [128, 128, 512], P(('group', 'shard')), may hold values from -6 to 6
- inner_projection_matrix: bfloat16 [1024, 1024], replicated, may hold values from -0.1875 to 0.1875
- student_rating_vector: bfloat16 [1024], replicated, may hold values from -0.1875 to 0.1875
- asking_matrix: bfloat16 [16, 1024, 512], P('shard'), may hold values from -0.1875 to 0.1875
- lookup_matrix: bfloat16 [16, 512, 512], P('shard'), may hold values from -0.25 to 0.25
- content_matrix: bfloat16 [16, 512, 512], P('shard'), may hold values from -0.25 to 0.25
- expert_rating_vector: bfloat16 [16, 512], P('shard'), may hold values from -1.1953125 to 1.1953125
Outputs:
- grad_hidden: float32 [1024, 1024], P('shard')
- grad_score: float32 [1024], replicated
Inputs may be any that keep to these rules, and one draw needn't show every extreme that they name: `kept_offers`: the 32 survivors of a request are distinct candidates. `expert_target`: each request names 6 distinct experts; the requests of one device name any expert at most 3 times, a bound that some block reaches.
All inputs are finite; a program needn't handle non-finite values.
Results may differ from a plain program's by a relative error of at most 0.005.
Values may be sent and summed in bfloat16 or wider, within the bound.
No kernel may reach another device: no remote copies, remote signals or barrier semaphores. Data moves between devices by JAX's collectives and lax.ppermute only.
A program may use at most 128 MiB of HBM per device.

v0:
```python
import jax
import jax.numpy as jnp
from jax import lax
from jax.sharding import PartitionSpec as P

ATTENDER_GANGS = 8


def body(
    offer_attribute_matrix,
    kept_offers,
    expert_target,
    sequence_extent,
    behaviour_sequence,
    inner_projection_matrix,
    student_rating_vector,
    asking_matrix,
    lookup_matrix,
    content_matrix,
    expert_rating_vector,
):
    requests_here, offer_number, attribute_span = offer_attribute_matrix.shape
    kept_number = kept_offers.shape[1]
    hist_slots, focus_span = (behaviour_sequence.shape[1], behaviour_sequence.shape[2])
    rankers_each = expert_target.shape[1]
    ranker_count = lax.axis_size("shard")
    routed_rows = requests_here * rankers_each
    capacity = max(2, (routed_rows + ranker_count - 1) // ranker_count + 1)
    place_number = ranker_count * capacity
    row_dest = expert_target.reshape(routed_rows)
    by_expert = (row_dest[:, None] == jnp.arange(ranker_count, dtype=jnp.int32)[None, :]).astype(
        jnp.int32
    )
    earlier = jnp.cumsum(by_expert, axis=0) - by_expert
    rank_in = jnp.sum(earlier * by_expert, axis=1)
    slot_of = row_dest * capacity + rank_in
    placing = slot_of[:, None] == jnp.arange(place_number, dtype=jnp.int32)[None, :]
    placing = placing.reshape(requests_here, rankers_each, place_number)
    placing_b = placing.astype(jnp.bfloat16)
    placing_f = placing.astype(jnp.float32)
    chosen_lines = (
        kept_offers[:, :, None] == jnp.arange(offer_number, dtype=jnp.int32)[None, None, :]
    ).astype(jnp.bfloat16)
    chosen = jnp.einsum(
        "rkc,rcf->rkf", chosen_lines, offer_attribute_matrix, preferred_element_type=jnp.float32
    ).astype(jnp.bfloat16)
    send_rows = jnp.einsum(
        "rts,rkf->skf", placing_b, chosen, preferred_element_type=jnp.float32
    ).astype(jnp.bfloat16)
    send_hist = jnp.einsum(
        "rts,rjf->sjf", placing_b, behaviour_sequence, preferred_element_type=jnp.float32
    ).astype(jnp.bfloat16)
    send_len = jnp.einsum("rts,r->s", placing_f, sequence_extent.astype(jnp.float32)).astype(
        jnp.bfloat16
    )
    arriving_lines, recv_hist, recv_len = (
        lax.all_to_all(send_rows, "shard", split_axis=0, concat_axis=0, tiled=True),
        lax.all_to_all(send_hist, "shard", split_axis=0, concat_axis=0, tiled=True),
        lax.all_to_all(send_len, "shard", split_axis=0, concat_axis=0, tiled=True),
    )
    single_attender_span = focus_span // ATTENDER_GANGS
    segment_places = 16
    segment_number = place_number // segment_places

    def ranker_block(block):
        rows, hist_rows, lens = block
        queries = jnp.dot(
            rows.reshape(-1, attribute_span), asking_matrix[0], preferred_element_type=jnp.float32
        )
        queries = queries.astype(jnp.bfloat16).reshape(
            segment_places, kept_number, ATTENDER_GANGS, single_attender_span
        )
        flat_hist = hist_rows.reshape(-1, focus_span)
        key_rows = jnp.dot(flat_hist, lookup_matrix[0], preferred_element_type=jnp.float32)
        key_rows = key_rows.astype(jnp.bfloat16).reshape(
            segment_places, hist_slots, ATTENDER_GANGS, single_attender_span
        )
        value_rows = jnp.dot(flat_hist, content_matrix[0], preferred_element_type=jnp.float32)
        value_rows = value_rows.astype(jnp.bfloat16).reshape(
            segment_places, hist_slots, ATTENDER_GANGS, single_attender_span
        )
        logits = jnp.einsum(
            "skhd,sjhd->shkj", queries, key_rows, preferred_element_type=jnp.float32
        ) * single_attender_span ** (-0.5)
        lengths = jnp.maximum(lens.astype(jnp.float32), jnp.float32(1.0))
        visible = (
            jnp.arange(hist_slots, dtype=jnp.float32)[None, None, None, :]
            < lengths[:, None, None, None]
        )
        weights = jnp.where(visible, jnp.exp(logits), jnp.float32(0.0))
        attn_probs = (weights / jnp.sum(weights, axis=-1, keepdims=True)).astype(jnp.bfloat16)
        mixed_context = jnp.einsum(
            "shkj,sjhd->skhd", attn_probs, value_rows, preferred_element_type=jnp.float32
        )
        mixed_context = mixed_context.reshape(segment_places, kept_number, focus_span)
        return jnp.sum(mixed_context * expert_rating_vector[0].astype(jnp.float32), axis=-1)

    mentor_output = lax.map(
        ranker_block,
        (
            arriving_lines.reshape(segment_number, segment_places, kept_number, attribute_span),
            recv_hist.reshape(segment_number, segment_places, hist_slots, focus_span),
            recv_len.reshape(segment_number, segment_places),
        ),
    )
    mentor_output = mentor_output.reshape(place_number, kept_number)
    returned = lax.all_to_all(mentor_output, "shard", split_axis=0, concat_axis=0, tiled=True)
    own_teacher = (
        jnp.einsum("rts,sk->rk", placing_f, returned, precision=lax.Precision.HIGHEST)
        / rankers_each
    )
    score_vec = student_rating_vector.astype(jnp.float32)
    flat_feats = offer_attribute_matrix.reshape(requests_here * offer_number, attribute_span)
    preact = jnp.dot(flat_feats, inner_projection_matrix, preferred_element_type=jnp.float32)
    hidden = jnp.maximum(preact, jnp.float32(0.0))
    scores = jnp.sum(hidden * score_vec, axis=-1).reshape(requests_here, offer_number)
    exp_scores = jnp.exp(scores)
    student = exp_scores / jnp.sum(exp_scores, axis=-1, keepdims=True)
    exp_teacher = jnp.exp(own_teacher)
    target = exp_teacher / jnp.sum(exp_teacher, axis=-1, keepdims=True)
    target_cand = jnp.sum(target[:, :, None] * chosen_lines.astype(jnp.float32), axis=1)
    score_grad = (student - target_cand).reshape(requests_here * offer_number, 1)
    hidden_grad = (score_grad * score_vec * (preact > 0).astype(jnp.float32)).astype(jnp.bfloat16)
    local_score = jnp.sum(score_grad * hidden, axis=0)
    grad_rows = lax.psum_scatter(
        lax.dot_general(
            flat_feats, hidden_grad, (((0,), (0,)), ((), ())), preferred_element_type=jnp.float32
        ),
        "shard",
        scatter_dimension=0,
        tiled=True,
    )
    grad_hidden = lax.psum(grad_rows, "group")
    grad_score = lax.psum(local_score, ("group", "shard"))
    return (grad_hidden, grad_score)


def solution(mesh):
    placed = (
        P(("group", "shard"), None, None),
        P(("group", "shard"), None),
        P(("group", "shard"), None),
        P(("group", "shard")),
        P(("group", "shard"), None, None),
        P(),
        P(),
        P("shard", None, None),
        P("shard", None, None),
        P("shard", None, None),
        P("shard", None),
    )
    return jax.shard_map(
        body, mesh=mesh, in_specs=placed, out_specs=(P("shard", None), P()), check_vma=False
    )
```

profile of v0, /device:TPU:0, one launch (start us, length us, event | category | flops | bytes accessed | tf_op | source)
XLA Modules:
  0.0 495.7 jit_solution(17073846660387039856)
XLA Ops:
  10.8 7.4 %all-to-all-start.1 = ((bf16[16,3,1]{1,2,0:T(2,128)(2,1)}), bf16[16,3,1]{1,2,0:T(2,128)(2,1)S(1)}, u32[]{:S(2)}, u32[]{:S(2)}) async-start(bf16[16,3,1]{1,2,0:T(2,128)(2,1)} %all_to_all.27), calls=%async_computation.1 | async-start | bytes 16384 | tf_op jit(solution)/shard_map/all_to_all | solution.py:59
  24.6 5.8 %all-to-all-start.2 = ((bf16[48,32,1024]{2,1,0:T(8,128)(2,1)}), bf16[48,32,1024]{2,1,0:T(8,128)(2,1)}, u32[]{:S(2)}, u32[]{:S(2)}) async-start(bf16[48,32,1024]{2,1,0:T(8,128)(2,1)} %copy.50), calls=%async_computation.2 | async-start | bytes 6291456 | tf_op jit(solution)/shard_map/all_to_all | solution.py:57
  32.3 6.3 %copy.47 = bf16[48,128,512]{2,1,0:T(8,128)(2,1)} copy(bf16[48,128,512]{2,0,1:T(8,128)(2,1)S(1)} %convolution_convert_fusion.3) | data formatting | bytes 12582912 | tf_op jit(solution)/shard_map/convert_element_type | solution.py:52
  38.6 51.1 %all-to-all-done.2 = bf16[48,32,1024]{2,1,0:T(8,128)(2,1)} async-done(((bf16[48,32,1024]{2,1,0:T(8,128)(2,1)}), bf16[48,32,1024]{2,1,0:T(8,128)(2,1)}, u32[]{:S(2)}, u32[]{:S(2)}) %all-to-all-start.2) | async-done | bytes 3145760 | tf_op jit(solution)/shard_map/all_to_all | solution.py:57
  89.7 15.5 %all-to-all-start = ((bf16[48,128,512]{2,1,0:T(8,128)(2,1)}), bf16[48,128,512]{2,1,0:T(8,128)(2,1)}, u32[]{:S(2)}, u32[]{:S(2)}) async-start(bf16[48,128,512]{2,1,0:T(8,128)(2,1)} %copy.47), calls=%async_computation | async-start | bytes 12582912 | tf_op jit(solution)/shard_map/all_to_all | solution.py:58
  108.0 111.3 %all-to-all-done = bf16[48,128,512]{2,1,0:T(8,128)(2,1)} async-done(((bf16[48,128,512]{2,1,0:T(8,128)(2,1)}), bf16[48,128,512]{2,1,0:T(8,128)(2,1)}, u32[]{:S(2)}, u32[]{:S(2)}) %all-to-all-start) | async-done | bytes 6291488 | tf_op jit(solution)/shard_map/all_to_all | solution.py:58
  219.3 107.4 %while.10 = (s32[]{:T(128)}, f32[3,16,32]{2,1,0:T(8,128)S(1)}, bf16[3,16,128,512]{3,2,1,0:T(8,128)(2,1)}, bf16[1,512,512]{2,1,0:T(8,128)(2,1)}, bf16[3,16]{1,0:T...) while((s32[]{:T(128)}, f32[3,16,32]{2,1,0:T(8,128)S(1)}, ...), condition=%wide.region_9.10_spmd, body=%wide.region_6.9_spmd.sunk | while | flops 2825123840 | bytes 61932960 | solution.py:98
  225.1 6.2 %reshape.149 = bf16[16,128,8,64]{3,2,1,0:T(8,128)(2,1)} reshape(bf16[2048,512]{1,0:T(8,128)(2,1)} %convolution_convert_fusion.10) | data formatting | bytes 4194304 | tf_op jit(solution)/shard_map/while/body/eval_jaxpr/reshape | solution.py:75
  236.0 6.0 %fusion.64 = (f32[16,8,32]{2,1,0:T(8,128)S(1)}, f32[16,8,32,128]{3,2,1,0:T(8,128)}) fusion(pred[16,128]{1,0:T(8,128)(4,1)S(1)} %iota_compare_fusion.6, bf16[16,128,8,64]{3,2,1,0:T(8,128)(2,1)} %reshape.149, bf16[16,32,8,64]{3,2,1,0:T(8,128)(2,1)S(1)} %reshape.150), kind=kOutput, calls=%fused_computation.9.clone.1 | convolution fusion | flops 68677632 | bytes 4737024 | tf_op jit(solution)/shard_map/while/body/eval_jaxpr/skhd,sjhd->shkj/dot_general | solution.py:82
  244.6 6.2 %reshape.148 = bf16[16,128,8,64]{3,2,1,0:T(8,128)(2,1)} reshape(bf16[2048,512]{1,0:T(8,128)(2,1)} %convolution_convert_fusion.9) | data formatting | bytes 4194304 | tf_op jit(solution)/shard_map/while/body/eval_jaxpr/reshape | solution.py:79
  260.8 6.2 %reshape.149 = bf16[16,128,8,64]{3,2,1,0:T(8,128)(2,1)} reshape(bf16[2048,512]{1,0:T(8,128)(2,1)} %convolution_convert_fusion.10) | data formatting | bytes 4194304 | tf_op jit(solution)/shard_map/while/body/eval_jaxpr/reshape | solution.py:75
  271.8 6.0 %fusion.64 = (f32[16,8,32]{2,1,0:T(8,128)S(1)}, f32[16,8,32,128]{3,2,1,0:T(8,128)}) fusion(pred[16,128]{1,0:T(8,128)(4,1)S(1)} %iota_compare_fusion.6, bf16[16,128,8,64]{3,2,1,0:T(8,128)(2,1)} %reshape.149, bf16[16,32,8,64]{3,2,1,0:T(8,128)(2,1)S(1)} %reshape.150), kind=kOutput, calls=%fused_computation.9.clone.1 | convolution fusion | flops 68677632 | bytes 4737024 | tf_op jit(solution)/shard_map/while/body/eval_jaxpr/skhd,sjhd->shkj/dot_general | solution.py:82
  280.4 6.2 %reshape.148 = bf16[16,128,8,64]{3,2,1,0:T(8,128)(2,1)} reshape(bf16[2048,512]{1,0:T(8,128)(2,1)} %convolution_convert_fusion.9) | data formatting | bytes 4194304 | tf_op jit(solution)/shard_map/while/body/eval_jaxpr/reshape | solution.py:79
  286.6 4.2 multiply_reduce_fusion.5
  296.6 6.2 %reshape.149 = bf16[16,128,8,64]{3,2,1,0:T(8,128)(2,1)} reshape(bf16[2048,512]{1,0:T(8,128)(2,1)} %convolution_convert_fusion.10) | data formatting | bytes 4194304 | tf_op jit(solution)/shard_map/while/body/eval_jaxpr/reshape | solution.py:75
  307.6 6.0 %fusion.64 = (f32[16,8,32]{2,1,0:T(8,128)S(1)}, f32[16,8,32,128]{3,2,1,0:T(8,128)}) fusion(pred[16,128]{1,0:T(8,128)(4,1)S(1)} %iota_compare_fusion.6, bf16[16,128,8,64]{3,2,1,0:T(8,128)(2,1)} %reshape.149, bf16[16,32,8,64]{3,2,1,0:T(8,128)(2,1)S(1)} %reshape.150), kind=kOutput, calls=%fused_computation.9.clone.1 | convolution fusion | flops 68677632 | bytes 4737024 | tf_op jit(solution)/shard_map/while/body/eval_jaxpr/skhd,sjhd->shkj/dot_general | solution.py:82
  316.2 6.2 %reshape.148 = bf16[16,128,8,64]{3,2,1,0:T(8,128)(2,1)} reshape(bf16[2048,512]{1,0:T(8,128)(2,1)} %convolution_convert_fusion.9) | data formatting | bytes 4194304 | tf_op jit(solution)/shard_map/while/body/eval_jaxpr/reshape | solution.py:79
  322.4 4.2 multiply_reduce_fusion.5
  327.3 28.1 %all-to-all-start.3 = ((f32[16,3,32]{2,1,0:T(4,128)}), f32[16,3,32]{2,1,0:T(4,128)S(1)}, u32[]{:S(2)}, u32[]{:S(2)}) async-start(f32[16,3,32]{2,1,0:T(4,128)} %all_to_all.24), calls=%async_computation.3 | async-start | bytes 65536 | tf_op jit(solution)/shard_map/all_to_all | solution.py:107
  355.5 6.5 %all-to-all-done.3 = f32[16,3,32]{2,1,0:T(4,128)S(1)} async-done(((f32[16,3,32]{2,1,0:T(4,128)}), f32[16,3,32]{2,1,0:T(4,128)S(1)}, u32[]{:S(2)}, u32[]{:S(2)}) %all-to-all-start.3) | async-done | bytes 6176 | tf_op jit(solution)/shard_map/all_to_all | solution.py:107
  362.6 5.2 %convolution_bitcast_fusion = f32[1024,1024]{0,1:T(8,128)} fusion(bf16[512,1024]{1,0:T(8,128)(2,1)} %bitcast.74, f32[512,1024]{1,0:T(8,128)} %get-tuple-element.101, f32[512]{0:T(512)S(1)} %bitcast_subtract_fusion, f32[1024]{0:T(1024)S(1)} %convert_element_type.71), kind=kOutput, calls=%fused_computation.32 | convolution fusion | flops 1075838976 | bytes 7346176 | tf_op jit(solution)/shard_map/dot_general | solution.py:126
  367.8 5.3 %copy.56 = f32[1024,1024]{1,0:T(8,128)} copy(f32[1024,1024]{0,1:T(8,128)} %convolution_bitcast_fusion) | data formatting | bytes 8388608
  373.2 70.1 %reduce-scatter.4.cloned.1.call-done = f32[64,1024]{1,0:T(8,128)} async-done(((f32[1024,1024]{1,0:T(8,128)}), f32[64,1024]{1,0:T(8,128)}) %reduce-scatter.4.cloned.1.call-update) | async-done | bytes 262160
  447.2 39.8 %psum.15 = f32[1024]{0:T(1024)} all-reduce(f32[1024]{0:T(1024)S(1)} %multiply_reduce_fusion.1), channel_id=1, replica_groups=mesh['group'=2,'shard'=16] {'group','shard'}, use_global_device_ids=true, to_apply=%region_15.16 | all-reduce | flops 1024 | bytes 8192 | tf_op jit(solution)/shard_map/psum | solution.py:134
  (111 shorter events, 65.6 us)
Async XLA Ops:
  7.2 98.1 %copy-start = (bf16[1024,1024]{1,0:T(8,128)(2,1)S(1)}, bf16[1024,1024]{1,0:T(8,128)(2,1)}, u32[]{:S(2)}) copy-start(bf16[1024,1024]{1,0:T(8,128)(2,1)} %param.18) | copy-start | bytes 6291460
  10.8 13.8 %all-to-all-start.1 = ((bf16[16,3,1]{1,2,0:T(2,128)(2,1)}), bf16[16,3,1]{1,2,0:T(2,128)(2,1)S(1)}, u32[]{:S(2)}, u32[]{:S(2)}) async-start(bf16[16,3,1]{1,2,0:T(2,128)(2,1)} %all_to_all.27), calls=%async_computation.1 | async-start | bytes 16384 | tf_op jit(solution)/shard_map/all_to_all | solution.py:59
  24.2 6.2 %copy-start.4 = (bf16[4,128,512]{2,1,0:T(8,128)(2,1)S(1)}, bf16[4,128,512]{2,1,0:T(8,128)(2,1)}, u32[]{:S(2)}) copy-start(bf16[4,128,512]{2,1,0:T(8,128)(2,1)} %param.17) | copy-start | bytes 1572868
  24.6 65.1 %all-to-all-start.2 = ((bf16[48,32,1024]{2,1,0:T(8,128)(2,1)}), bf16[48,32,1024]{2,1,0:T(8,128)(2,1)}, u32[]{:S(2)}, u32[]{:S(2)}) async-start(bf16[48,32,1024]{2,1,0:T(8,128)(2,1)} %copy.50), calls=%async_computation.2 | async-start | bytes 6291456 | tf_op jit(solution)/shard_map/all_to_all | solution.py:57
  38.6 66.6 %copy-start.7 = (bf16[1024]{0:T(1024)(128)(2,1)S(1)}, bf16[1024]{0:T(1024)(128)(2,1)}, u32[]{:S(2)}) copy-start(bf16[1024]{0:T(1024)(128)(2,1)} %param.19) | copy-start | bytes 6148
  38.6 66.7 %copy-start.3 = (bf16[4,128,1024]{2,1,0:T(8,128)(2,1)S(1)}, bf16[4,128,1024]{2,1,0:T(8,128)(2,1)}, u32[]{:S(2)}) copy-start(bf16[4,128,1024]{2,1,0:T(8,128)(2,1)} %param.13) | copy-start | bytes 3145732
  89.7 129.5 %all-to-all-start = ((bf16[48,128,512]{2,1,0:T(8,128)(2,1)}), bf16[48,128,512]{2,1,0:T(8,128)(2,1)}, u32[]{:S(2)}, u32[]{:S(2)}) async-start(bf16[48,128,512]{2,1,0:T(8,128)(2,1)} %copy.47), calls=%async_computation | async-start | bytes 12582912 | tf_op jit(solution)/shard_map/all_to_all | solution.py:58
  105.3 114.0 %copy-start.5 = (bf16[1,512]{1,0:T(2,128)(2,1)S(1)}, bf16[1,512]{1,0:T(2,128)(2,1)}, u32[]{:S(2)}) copy-start(bf16[1,512]{1,0:T(2,128)(2,1)} %param.23) | copy-start | bytes 3076
  219.3 143.1 %copy-start.6 = (s32[4,32]{1,0:T(4,128)S(1)}, s32[4,32]{1,0:T(4,128)}, u32[]{:S(2)}) copy-start(s32[4,32]{1,0:T(4,128)} %param.14) | copy-start | bytes 1540
  219.3 3.2 copy-start.10
  231.2 1.5 copy-start.8
  236.0 6.0 %copy-start.2 = (bf16[1,16,128,512]{3,2,1,0:T(8,128)(2,1)S(1)}, bf16[1,16,128,512]{3,2,1,0:T(8,128)(2,1)}, u32[]{:S(2)}) copy-start(bf16[1,16,128,512]{3,2,1,0:T(8,128)(2,1)} %copy-done.1) | copy-start | bytes 6291460 | tf_op jit(solution)/shard_map/while
  236.0 6.0 %copy-start.9 = (bf16[1,512,512]{2,1,0:T(8,128)(2,1)S(1)}, bf16[1,512,512]{2,1,0:T(8,128)(2,1)}, u32[]{:S(2)}) copy-start(bf16[1,512,512]{2,1,0:T(8,128)(2,1)} %get-tuple-element.184) | copy-start | bytes 1572868 | tf_op jit(solution)/shard_map/while
  255.1 3.2 copy-start.10
  267.0 1.5 copy-start.8
  271.8 6.0 %copy-start.2 = (bf16[1,16,128,512]{3,2,1,0:T(8,128)(2,1)S(1)}, bf16[1,16,128,512]{3,2,1,0:T(8,128)(2,1)}, u32[]{:S(2)}) copy-start(bf16[1,16,128,512]{3,2,1,0:T(8,128)(2,1)} %copy-done.1) | copy-start | bytes 6291460 | tf_op jit(solution)/shard_map/while
  271.8 6.0 %copy-start.9 = (bf16[1,512,512]{2,1,0:T(8,128)(2,1)S(1)}, bf16[1,512,512]{2,1,0:T(8,128)(2,1)}, u32[]{:S(2)}) copy-start(bf16[1,512,512]{2,1,0:T(8,128)(2,1)} %get-tuple-element.184) | copy-start | bytes 1572868 | tf_op jit(solution)/shard_map/while
  290.9 3.2 copy-start.10
  302.8 1.5 copy-start.8
  307.6 6.0 %copy-start.2 = (bf16[1,16,128,512]{3,2,1,0:T(8,128)(2,1)S(1)}, bf16[1,16,128,512]{3,2,1,0:T(8,128)(2,1)}, u32[]{:S(2)}) copy-start(bf16[1,16,128,512]{3,2,1,0:T(8,128)(2,1)} %copy-done.1) | copy-start | bytes 6291460 | tf_op jit(solution)/shard_map/while
  307.6 6.0 %copy-start.9 = (bf16[1,512,512]{2,1,0:T(8,128)(2,1)S(1)}, bf16[1,512,512]{2,1,0:T(8,128)(2,1)}, u32[]{:S(2)}) copy-start(bf16[1,512,512]{2,1,0:T(8,128)(2,1)} %get-tuple-element.184) | copy-start | bytes 1572868 | tf_op jit(solution)/shard_map/while
  327.3 34.7 %all-to-all-start.3 = ((f32[16,3,32]{2,1,0:T(4,128)}), f32[16,3,32]{2,1,0:T(4,128)S(1)}, u32[]{:S(2)}, u32[]{:S(2)}) async-start(f32[16,3,32]{2,1,0:T(4,128)} %all_to_all.24), calls=%async_computation.3 | async-start | bytes 65536 | tf_op jit(solution)/shard_map/all_to_all | solution.py:107
  355.4 88.0 %reduce-scatter.4.cloned.1.call-start = ((), (), s32[]{:S(2)}) async-start(), calls=%async_computation.6 | async-start | bytes 4456448
  373.1 113.8 %all-reduce.2.cloned.1.call-start = ((), (), s32[]{:S(2)}) async-start(), calls=%async_computation.5 | async-start | bytes 1048576 | tf_op jit(solution)/shard_map/psum | solution.py:133
  (3 other events, 3.9 us)
Sparse Core Ops, SparseCore 0:
  373.3 70.0 reduce-scatter.3
  445.6 28.0 all-reduce.1
where the time goes:
time: 497 us; the launch traced here: 496 us
  waiting for transfers between devices  239 us (48%)
  local copies, waits for them, and re-layouts  77.7 us (16%)
  matrix products  63.9 us (13%)
  starting transfers between devices  56.9 us (11%)
  blocking collectives  39.8 us (8%)
  between operations  14.2 us (3%)
    all_to_all x1, waiting for transfers between devices, body(): lax.all_to_all(send_hist, 'shard', split_axis=0, concat_axis=0, tiled=True)  111 us
    unnamed x3, waiting for transfers between devices  70.2 us
    all_to_all x1, waiting for transfers between devices, body(): lax.all_to_all(send_rows, 'shard', split_axis=0, concat_axis=0, tiled=True)  51.1 us
    psum x1, blocking collectives, body(): grad_score = lax.psum(local_score, ('group', 'shard'))  39.8 us
    all_to_all x1, starting transfers between devices, body(): lax.all_to_all(mentor_output, 'shard', split_axis=0, concat_axis=0, tiled...  28.1 us
    reshape x3, local copies, waits for them, and re-layouts, ranker_block(): key_rows.astype(jnp.bfloat16)  18.5 us
    reshape x3, local copies, waits for them, and re-layouts, ranker_block(): value_rows.astype(jnp.bfloat16)  18.5 us
    dot_general x3, matrix products, ranker_block(): jnp.einsum('skhd,sjhd->shkj', queries, key_rows, preferred_element_type=j...  17.9 us
  transfers between devices with their start and end apart: 6, of which 5 were waited for; matrix products, arithmetic and copies ran while one was open for 4% of the time, Pallas kernels for 0%

commit v1 on v0

--- a/solution.py
+++ b/solution.py
@@ -131,7 +131,7 @@
         tiled=True,
     )
     grad_hidden = lax.psum(grad_rows, "group")
-    grad_score = lax.psum(local_score, ("group", "shard"))
+    grad_score = lax.psum(lax.psum(local_score, "shard"), "group")
     return (grad_hidden, grad_score)
 
 

time: 497 us -> 493 us (level)
    psum x1 -> x2, blocking collectives: 39.8 us -> 35 us  [body(): grad_score = lax.psum(lax.psum(local_score, 'shard'), 'group')]
where the time goes in v1:
time: 493 us; the launch traced here: 491 us
  waiting for transfers between devices  239 us (48%)
  local copies, waits for them, and re-layouts  77.7 us (16%)
  matrix products  63.9 us (13%)
  starting transfers between devices  56.9 us (12%)
  blocking collectives  35 us (7%)
  between operations  14.2 us (3%)
    all_to_all x1, waiting for transfers between devices, body(): lax.all_to_all(send_hist, 'shard', split_axis=0, concat_axis=0, tiled=True)  111 us
    unnamed x3, waiting for transfers between devices  70.2 us
    all_to_all x1, waiting for transfers between devices, body(): lax.all_to_all(send_rows, 'shard', split_axis=0, concat_axis=0, tiled=True)  51.1 us
    psum x2, blocking collectives, body(): grad_score = lax.psum(lax.psum(local_score, 'shard'), 'group')  35 us
    all_to_all x1, starting transfers between devices, body(): lax.all_to_all(mentor_output, 'shard', split_axis=0, concat_axis=0, tiled...  28.1 us
    reshape x3, local copies, waits for them, and re-layouts, ranker_block(): key_rows.astype(jnp.bfloat16)  18.5 us
    reshape x3, local copies, waits for them, and re-layouts, ranker_block(): value_rows.astype(jnp.bfloat16)  18.5 us
    dot_general x3, matrix products, ranker_block(): jnp.einsum('skhd,sjhd->shkj', queries, key_rows, preferred_element_type=j...  17.9 us
  transfers between devices with their start and end apart: 6, of which 5 were waited for; matrix products, arithmetic and copies ran while one was open for 4% of the time, Pallas kernels for 0%

profile of v1, /device:TPU:0, one launch (start us, length us, event | category | flops | bytes accessed | tf_op | source)
XLA Modules:
  0.0 490.9 jit_solution(278818853257562)
XLA Ops:
  10.8 7.4 %all-to-all-start.1 = ((bf16[16,3,1]{1,2,0:T(2,128)(2,1)}), bf16[16,3,1]{1,2,0:T(2,128)(2,1)S(1)}, u32[]{:S(2)}, u32[]{:S(2)}) async-start(bf16[16,3,1]{1,2,0:T(2,128)(2,1)} %all_to_all.27), calls=%async_computation.1 | async-start | bytes 16384 | tf_op jit(solution)/shard_map/all_to_all | solution.py:59
  24.6 5.8 %all-to-all-start.2 = ((bf16[48,32,1024]{2,1,0:T(8,128)(2,1)}), bf16[48,32,1024]{2,1,0:T(8,128)(2,1)}, u32[]{:S(2)}, u32[]{:S(2)}) async-start(bf16[48,32,1024]{2,1,0:T(8,128)(2,1)} %copy.50), calls=%async_computation.2 | async-start | bytes 6291456 | tf_op jit(solution)/shard_map/all_to_all | solution.py:57
  32.3 6.3 %copy.47 = bf16[48,128,512]{2,1,0:T(8,128)(2,1)} copy(bf16[48,128,512]{2,0,1:T(8,128)(2,1)S(1)} %convolution_convert_fusion.3) | data formatting | bytes 12582912 | tf_op jit(solution)/shard_map/convert_element_type | solution.py:52
  38.6 51.1 %all-to-all-done.2 = bf16[48,32,1024]{2,1,0:T(8,128)(2,1)} async-done(((bf16[48,32,1024]{2,1,0:T(8,128)(2,1)}), bf16[48,32,1024]{2,1,0:T(8,128)(2,1)}, u32[]{:S(2)}, u32[]{:S(2)}) %all-to-all-start.2) | async-done | bytes 3145760 | tf_op jit(solution)/shard_map/all_to_all | solution.py:57
  89.7 15.5 %all-to-all-start = ((bf16[48,128,512]{2,1,0:T(8,128)(2,1)}), bf16[48,128,512]{2,1,0:T(8,128)(2,1)}, u32[]{:S(2)}, u32[]{:S(2)}) async-start(bf16[48,128,512]{2,1,0:T(8,128)(2,1)} %copy.47), calls=%async_computation | async-start | bytes 12582912 | tf_op jit(solution)/shard_map/all_to_all | solution.py:58
  108.0 111.3 %all-to-all-done = bf16[48,128,512]{2,1,0:T(8,128)(2,1)} async-done(((bf16[48,128,512]{2,1,0:T(8,128)(2,1)}), bf16[48,128,512]{2,1,0:T(8,128)(2,1)}, u32[]{:S(2)}, u32[]{:S(2)}) %all-to-all-start) | async-done | bytes 6291488 | tf_op jit(solution)/shard_map/all_to_all | solution.py:58
  219.3 107.4 %while.10 = (s32[]{:T(128)}, f32[3,16,32]{2,1,0:T(8,128)S(1)}, bf16[3,16,128,512]{3,2,1,0:T(8,128)(2,1)}, bf16[1,512,512]{2,1,0:T(8,128)(2,1)}, bf16[3,16]{1,0:T...) while((s32[]{:T(128)}, f32[3,16,32]{2,1,0:T(8,128)S(1)}, ...), condition=%wide.region_9.10_spmd, body=%wide.region_6.9_spmd.sunk | while | flops 2825123840 | bytes 61932960 | solution.py:98
  225.1 6.2 %reshape.149 = bf16[16,128,8,64]{3,2,1,0:T(8,128)(2,1)} reshape(bf16[2048,512]{1,0:T(8,128)(2,1)} %convolution_convert_fusion.10) | data formatting | bytes 4194304 | tf_op jit(solution)/shard_map/while/body/eval_jaxpr/reshape | solution.py:75
  236.0 6.0 %fusion.64 = (f32[16,8,32]{2,1,0:T(8,128)S(1)}, f32[16,8,32,128]{3,2,1,0:T(8,128)}) fusion(pred[16,128]{1,0:T(8,128)(4,1)S(1)} %iota_compare_fusion.6, bf16[16,128,8,64]{3,2,1,0:T(8,128)(2,1)} %reshape.149, bf16[16,32,8,64]{3,2,1,0:T(8,128)(2,1)S(1)} %reshape.150), kind=kOutput, calls=%fused_computation.9.clone.1 | convolution fusion | flops 68677632 | bytes 4737024 | tf_op jit(solution)/shard_map/while/body/eval_jaxpr/skhd,sjhd->shkj/dot_general | solution.py:82
  244.6 6.2 %reshape.148 = bf16[16,128,8,64]{3,2,1,0:T(8,128)(2,1)} reshape(bf16[2048,512]{1,0:T(8,128)(2,1)} %convolution_convert_fusion.9) | data formatting | bytes 4194304 | tf_op jit(solution)/shard_map/while/body/eval_jaxpr/reshape | solution.py:79
  260.8 6.2 %reshape.149 = bf16[16,128,8,64]{3,2,1,0:T(8,128)(2,1)} reshape(bf16[2048,512]{1,0:T(8,128)(2,1)} %convolution_convert_fusion.10) | data formatting | bytes 4194304 | tf_op jit(solution)/shard_map/while/body/eval_jaxpr/reshape | solution.py:75
  271.8 6.0 %fusion.64 = (f32[16,8,32]{2,1,0:T(8,128)S(1)}, f32[16,8,32,128]{3,2,1,0:T(8,128)}) fusion(pred[16,128]{1,0:T(8,128)(4,1)S(1)} %iota_compare_fusion.6, bf16[16,128,8,64]{3,2,1,0:T(8,128)(2,1)} %reshape.149, bf16[16,32,8,64]{3,2,1,0:T(8,128)(2,1)S(1)} %reshape.150), kind=kOutput, calls=%fused_computation.9.clone.1 | convolution fusion | flops 68677632 | bytes 4737024 | tf_op jit(solution)/shard_map/while/body/eval_jaxpr/skhd,sjhd->shkj/dot_general | solution.py:82
  280.4 6.2 %reshape.148 = bf16[16,128,8,64]{3,2,1,0:T(8,128)(2,1)} reshape(bf16[2048,512]{1,0:T(8,128)(2,1)} %convolution_convert_fusion.9) | data formatting | bytes 4194304 | tf_op jit(solution)/shard_map/while/body/eval_jaxpr/reshape | solution.py:79
  286.6 4.2 multiply_reduce_fusion.5
  296.6 6.2 %reshape.149 = bf16[16,128,8,64]{3,2,1,0:T(8,128)(2,1)} reshape(bf16[2048,512]{1,0:T(8,128)(2,1)} %convolution_convert_fusion.10) | data formatting | bytes 4194304 | tf_op jit(solution)/shard_map/while/body/eval_jaxpr/reshape | solution.py:75
  307.6 6.0 %fusion.64 = (f32[16,8,32]{2,1,0:T(8,128)S(1)}, f32[16,8,32,128]{3,2,1,0:T(8,128)}) fusion(pred[16,128]{1,0:T(8,128)(4,1)S(1)} %iota_compare_fusion.6, bf16[16,128,8,64]{3,2,1,0:T(8,128)(2,1)} %reshape.149, bf16[16,32,8,64]{3,2,1,0:T(8,128)(2,1)S(1)} %reshape.150), kind=kOutput, calls=%fused_computation.9.clone.1 | convolution fusion | flops 68677632 | bytes 4737024 | tf_op jit(solution)/shard_map/while/body/eval_jaxpr/skhd,sjhd->shkj/dot_general | solution.py:82
  316.2 6.2 %reshape.148 = bf16[16,128,8,64]{3,2,1,0:T(8,128)(2,1)} reshape(bf16[2048,512]{1,0:T(8,128)(2,1)} %convolution_convert_fusion.9) | data formatting | bytes 4194304 | tf_op jit(solution)/shard_map/while/body/eval_jaxpr/reshape | solution.py:79
  327.3 28.1 %all-to-all-start.3 = ((f32[16,3,32]{2,1,0:T(4,128)}), f32[16,3,32]{2,1,0:T(4,128)S(1)}, u32[]{:S(2)}, u32[]{:S(2)}) async-start(f32[16,3,32]{2,1,0:T(4,128)} %all_to_all.24), calls=%async_computation.3 | async-start | bytes 65536 | tf_op jit(solution)/shard_map/all_to_all | solution.py:107
  355.5 6.5 %all-to-all-done.3 = f32[16,3,32]{2,1,0:T(4,128)S(1)} async-done(((f32[16,3,32]{2,1,0:T(4,128)}), f32[16,3,32]{2,1,0:T(4,128)S(1)}, u32[]{:S(2)}, u32[]{:S(2)}) %all-to-all-start.3) | async-done | bytes 6176 | tf_op jit(solution)/shard_map/all_to_all | solution.py:107
  362.6 5.2 %convolution_bitcast_fusion = f32[1024,1024]{0,1:T(8,128)} fusion(bf16[512,1024]{1,0:T(8,128)(2,1)} %bitcast.74, f32[512,1024]{1,0:T(8,128)} %get-tuple-element.101, f32[512]{0:T(512)S(1)} %bitcast_subtract_fusion, f32[1024]{0:T(1024)S(1)} %convert_element_type.71), kind=kOutput, calls=%fused_computation.32 | convolution fusion | flops 1075838976 | bytes 7346176 | tf_op jit(solution)/shard_map/dot_general | solution.py:126
  367.8 5.3 %copy.56 = f32[1024,1024]{1,0:T(8,128)} copy(f32[1024,1024]{0,1:T(8,128)} %convolution_bitcast_fusion) | data formatting | bytes 8388608
  373.2 70.1 %reduce-scatter.4.cloned.1.call-done = f32[64,1024]{1,0:T(8,128)} async-done(((f32[1024,1024]{1,0:T(8,128)}), f32[64,1024]{1,0:T(8,128)}) %reduce-scatter.4.cloned.1.call-update) | async-done | bytes 262160
  447.2 29.5 %psum.22 = f32[1024]{0:T(1024)S(1)} all-reduce(f32[1024]{0:T(1024)S(1)} %multiply_reduce_fusion.1), channel_id=1, replica_groups=mesh['group'=2,'shard'=16] {'shard'}, use_global_device_ids=true, to_apply=%region_15.16 | all-reduce | flops 1024 | bytes 8192 | tf_op jit(solution)/shard_map/psum | solution.py:134
  476.7 5.5 %psum.23 = f32[1024]{0:T(1024)} all-reduce(f32[1024]{0:T(1024)S(1)} %psum.22), channel_id=1, replica_groups=mesh['group'=2,'shard'=16] {'group'}, use_global_device_ids=true, to_apply=%region_16.17 | all-reduce | flops 1024 | bytes 8192 | tf_op jit(solution)/shard_map/psum | solution.py:134
  (112 shorter events, 69.8 us)
Async XLA Ops:
  7.2 98.1 %copy-start = (bf16[1024,1024]{1,0:T(8,128)(2,1)S(1)}, bf16[1024,1024]{1,0:T(8,128)(2,1)}, u32[]{:S(2)}) copy-start(bf16[1024,1024]{1,0:T(8,128)(2,1)} %param.18) | copy-start | bytes 6291460
  10.8 13.8 %all-to-all-start.1 = ((bf16[16,3,1]{1,2,0:T(2,128)(2,1)}), bf16[16,3,1]{1,2,0:T(2,128)(2,1)S(1)}, u32[]{:S(2)}, u32[]{:S(2)}) async-start(bf16[16,3,1]{1,2,0:T(2,128)(2,1)} %all_to_all.27), calls=%async_computation.1 | async-start | bytes 16384 | tf_op jit(solution)/shard_map/all_to_all | solution.py:59
  24.2 6.2 %copy-start.4 = (bf16[4,128,512]{2,1,0:T(8,128)(2,1)S(1)}, bf16[4,128,512]{2,1,0:T(8,128)(2,1)}, u32[]{:S(2)}) copy-start(bf16[4,128,512]{2,1,0:T(8,128)(2,1)} %param.17) | copy-start | bytes 1572868
  24.6 65.1 %all-to-all-start.2 = ((bf16[48,32,1024]{2,1,0:T(8,128)(2,1)}), bf16[48,32,1024]{2,1,0:T(8,128)(2,1)}, u32[]{:S(2)}, u32[]{:S(2)}) async-start(bf16[48,32,1024]{2,1,0:T(8,128)(2,1)} %copy.50), calls=%async_computation.2 | async-start | bytes 6291456 | tf_op jit(solution)/shard_map/all_to_all | solution.py:57
  38.6 66.6 %copy-start.7 = (bf16[1024]{0:T(1024)(128)(2,1)S(1)}, bf16[1024]{0:T(1024)(128)(2,1)}, u32[]{:S(2)}) copy-start(bf16[1024]{0:T(1024)(128)(2,1)} %param.19) | copy-start | bytes 6148
  38.6 66.7 %copy-start.3 = (bf16[4,128,1024]{2,1,0:T(8,128)(2,1)S(1)}, bf16[4,128,1024]{2,1,0:T(8,128)(2,1)}, u32[]{:S(2)}) copy-start(bf16[4,128,1024]{2,1,0:T(8,128)(2,1)} %param.13) | copy-start | bytes 3145732
  89.7 129.5 %all-to-all-start = ((bf16[48,128,512]{2,1,0:T(8,128)(2,1)}), bf16[48,128,512]{2,1,0:T(8,128)(2,1)}, u32[]{:S(2)}, u32[]{:S(2)}) async-start(bf16[48,128,512]{2,1,0:T(8,128)(2,1)} %copy.47), calls=%async_computation | async-start | bytes 12582912 | tf_op jit(solution)/shard_map/all_to_all | solution.py:58
  105.3 114.0 %copy-start.5 = (bf16[1,512]{1,0:T(2,128)(2,1)S(1)}, bf16[1,512]{1,0:T(2,128)(2,1)}, u32[]{:S(2)}) copy-start(bf16[1,512]{1,0:T(2,128)(2,1)} %param.23) | copy-start | bytes 3076
  219.3 143.1 %copy-start.6 = (s32[4,32]{1,0:T(4,128)S(1)}, s32[4,32]{1,0:T(4,128)}, u32[]{:S(2)}) copy-start(s32[4,32]{1,0:T(4,128)} %param.14) | copy-start | bytes 1540
  219.3 3.2 copy-start.10
  231.2 1.5 copy-start.8
  236.0 6.0 %copy-start.2 = (bf16[1,16,128,512]{3,2,1,0:T(8,128)(2,1)S(1)}, bf16[1,16,128,512]{3,2,1,0:T(8,128)(2,1)}, u32[]{:S(2)}) copy-start(bf16[1,16,128,512]{3,2,1,0:T(8,128)(2,1)} %copy-done.1) | copy-start | bytes 6291460 | tf_op jit(solution)/shard_map/while
  236.0 6.0 %copy-start.9 = (bf16[1,512,512]{2,1,0:T(8,128)(2,1)S(1)}, bf16[1,512,512]{2,1,0:T(8,128)(2,1)}, u32[]{:S(2)}) copy-start(bf16[1,512,512]{2,1,0:T(8,128)(2,1)} %get-tuple-element.184) | copy-start | bytes 1572868 | tf_op jit(solution)/shard_map/while
  255.1 3.2 copy-start.10
  267.0 1.5 copy-start.8
  271.8 6.0 %copy-start.2 = (bf16[1,16,128,512]{3,2,1,0:T(8,128)(2,1)S(1)}, bf16[1,16,128,512]{3,2,1,0:T(8,128)(2,1)}, u32[]{:S(2)}) copy-start(bf16[1,16,128,512]{3,2,1,0:T(8,128)(2,1)} %copy-done.1) | copy-start | bytes 6291460 | tf_op jit(solution)/shard_map/while
  271.8 6.0 %copy-start.9 = (bf16[1,512,512]{2,1,0:T(8,128)(2,1)S(1)}, bf16[1,512,512]{2,1,0:T(8,128)(2,1)}, u32[]{:S(2)}) copy-start(bf16[1,512,512]{2,1,0:T(8,128)(2,1)} %get-tuple-element.184) | copy-start | bytes 1572868 | tf_op jit(solution)/shard_map/while
  290.9 3.2 copy-start.10
  302.8 1.5 copy-start.8
  307.6 6.0 %copy-start.2 = (bf16[1,16,128,512]{3,2,1,0:T(8,128)(2,1)S(1)}, bf16[1,16,128,512]{3,2,1,0:T(8,128)(2,1)}, u32[]{:S(2)}) copy-start(bf16[1,16,128,512]{3,2,1,0:T(8,128)(2,1)} %copy-done.1) | copy-start | bytes 6291460 | tf_op jit(solution)/shard_map/while
  307.6 6.0 %copy-start.9 = (bf16[1,512,512]{2,1,0:T(8,128)(2,1)S(1)}, bf16[1,512,512]{2,1,0:T(8,128)(2,1)}, u32[]{:S(2)}) copy-start(bf16[1,512,512]{2,1,0:T(8,128)(2,1)} %get-tuple-element.184) | copy-start | bytes 1572868 | tf_op jit(solution)/shard_map/while
  327.3 34.7 %all-to-all-start.3 = ((f32[16,3,32]{2,1,0:T(4,128)}), f32[16,3,32]{2,1,0:T(4,128)S(1)}, u32[]{:S(2)}, u32[]{:S(2)}) async-start(f32[16,3,32]{2,1,0:T(4,128)} %all_to_all.24), calls=%async_computation.3 | async-start | bytes 65536 | tf_op jit(solution)/shard_map/all_to_all | solution.py:107
  355.4 88.0 %reduce-scatter.4.cloned.1.call-start = ((), (), s32[]{:S(2)}) async-start(), calls=%async_computation.6 | async-start | bytes 4456448
  373.1 109.0 %all-reduce.2.cloned.1.call-start = ((), (), s32[]{:S(2)}) async-start(), calls=%async_computation.5 | async-start | bytes 1048576 | tf_op jit(solution)/shard_map/psum | solution.py:133
  (3 other events, 3.9 us)
Sparse Core Ops, SparseCore 0:
  373.3 70.0 reduce-scatter.3
  445.6 27.6 all-reduce.1
